TPU v7x, 512 devices: a whole 4x4x16 slice. The times are simulated.
512 devices in a mesh: seq: 64 (over y, z), mp: 8 (over x, core).
Axes of the slice: x: 4, y: 4, z: 16, core: 2. Of those that a mesh axis runs over, the one named last changes fastest.
Arguments:
- byte_states: bfloat16 [16384, 1024], P('seq'), may hold values from -6 to 6
- outer_gain: float32 [1024], replicated, may hold values from 0.1 to 1.9
- mamba_input: bfloat16 [1024, 1024], P(None, 'mp'), may hold values from -0.1875 to 0.1875
- mamba_step: bfloat16 [1024, 1024], P(None, 'mp'), may hold values from -0.1875 to 0.1875
- decay_rate: float32 [1024], P('mp'), as said below
- mixer_weight: bfloat16 [1024, 1024], P('mp'), may hold values from -0.1875 to 0.1875
- boundaries: int32 [64, 128], P('seq'), may hold values from 0 to 256, as said below
- span_counts: int32 [64], replicated, may hold values from 1 to 128, as said below
- up_weight: bfloat16 [1024, 4096], P('seq', 'mp'), may hold values from -0.1875 to 0.1875
- up_bias: float32 [4096], P('mp'), may hold values from -5 to 5
- inner_gain: float32 [4096], replicated, as said below
- query_weight: bfloat16 [4096, 4096], P('seq', 'mp'), as said below
- key_weight: bfloat16 [4096, 1024], P('seq', 'mp'), as said below
- value_weight: bfloat16 [4096, 1024], P('seq', 'mp'), may hold values from -0.09375 to 0.09375
- return_weight: bfloat16 [4096, 1024], P('mp'), may hold values from -0.09375 to 0.09375
Outputs:
- joined: bfloat16 [16384, 1024], P('seq', 'mp')
Inputs may be any that keep to these rules, and one draw needn't show every extreme that they name: `boundaries`: row s lists the spans of shard s: its first span_counts[s] entries rise strictly from 0 and are byte positions within the shard; each span runs to the next entry, the last to the shard's end; the other entries equal 256. `span_counts`: the counts sum to 4096; some shard has exactly 128 spans. `decay_rate`: Positive. `inner_gain`: Positive. `query_weight`: Finite. `key_weight`: Finite.
All inputs are finite; a program needn't handle non-finite values.
Results may differ from a plain program's by a relative error of at most 0.01.
Values may be sent and summed in bfloat16 or wider, within the bound.
A program may use at most 64 MiB of HBM per device.

v0:
```python
import math
import jax
import jax.numpy as jnp
from jax import lax
from jax.sharding import PartitionSpec as P

HEADS = 32
KV_HEADS = 8
HEAD = 128
eps = 1e-05
masked = -1e30
far_index = 1073741824


def prefix(value, axis, join, neutral):
    count, mine = (lax.axis_size(axis), lax.axis_index(axis))
    pieces = jax.tree.map(lambda part: lax.all_gather(part, axis), value)
    so_far = jax.tree.map(
        lambda part, zero: jnp.full_like(part, 0) + jnp.asarray(zero, part.dtype), value, neutral
    )

    def lap(position, so_far):
        longer = join(so_far, jax.tree.map(lambda part: part[position], pieces))
        return jax.tree.map(lambda new, old: jnp.where(position < mine, new, old), longer, so_far)

    return lax.fori_loop(0, count - 1, lap, so_far)


def rms_scale(values, gain):
    values = values.astype(jnp.float32)
    return values * lax.rsqrt(jnp.mean(values * values, axis=-1, keepdims=True) + eps) * gain


def combine_pairs(earlier, later):
    return (earlier[0] * later[0], later[0] * earlier[1] + later[1])


def pick_table(table, wanted, seq_ids):
    return jnp.sum(jnp.where(seq_ids[None, :] == wanted[:, None], table[None, :], 0), axis=1)


def block_size(piece_rows, shard_rows):
    limit = max(1, 1024 // shard_rows)
    pieces = max(1, piece_rows // shard_rows)
    best_size = 1
    for candidate in range(1, limit + 1):
        if pieces % candidate == 0:
            best_size = candidate
    return min(piece_rows, best_size * shard_rows)


def on_device(
    byte_states,
    outer_gain,
    mamba_input,
    mamba_step,
    decay_rate,
    mixer_weight,
    boundaries,
    span_counts,
    up_weight,
    up_bias,
    inner_gain,
    query_weight,
    key_weight,
    value_weight,
    return_weight,
):
    shards = lax.axis_size("seq")
    own_shard = lax.axis_index("seq")
    own_lane = lax.axis_index("mp")
    rows_here = byte_states.shape[0]
    capacity = boundaries.shape[1]
    column_count = mamba_input.shape[1]
    kv_local = key_weight.shape[1] // HEAD
    group_size = HEADS // KV_HEADS
    offsets = jnp.cumsum(span_counts) - span_counts
    seq_ids = jnp.arange(shards, dtype=jnp.int32)
    own_offset = jnp.sum(jnp.where(seq_ids == own_shard, offsets, 0))
    own_count = jnp.sum(jnp.where(seq_ids == own_shard, span_counts, 0))
    normed = rms_scale(byte_states, outer_gain).astype(jnp.bfloat16)
    inputs = jnp.dot(normed, mamba_input, preferred_element_type=jnp.float32)
    step_sizes = jax.nn.softplus(jnp.dot(normed, mamba_step, preferred_element_type=jnp.float32))
    rate_steps = step_sizes * decay_rate
    decays = jnp.exp(-rate_steps)
    drives = jnp.sqrt(-jnp.expm1(-2.0 * rate_steps)) * inputs
    through, local_states = lax.associative_scan(combine_pairs, (decays, drives), axis=0)
    starting = (jnp.ones((column_count,), jnp.float32), jnp.zeros((column_count,), jnp.float32))
    arriving = prefix((through[-1], local_states[-1]), "seq", combine_pairs, starting)
    states = (local_states + through * arriving[1][None, :]).astype(jnp.bfloat16)
    partial_value = jnp.dot(states, mixer_weight, preferred_element_type=jnp.float32)
    mixed_sum = lax.psum(partial_value, "mp")
    encoded = (byte_states.astype(jnp.float32) + mixed_sum).astype(jnp.bfloat16)
    skip_part = lax.dynamic_slice_in_dim(encoded, own_lane * column_count, column_count, 1)
    own_marks = boundaries[0]
    pooled = encoded[jnp.minimum(own_marks, rows_here - 1)]
    local_slot = jnp.arange(capacity, dtype=jnp.int32)
    query_index = jnp.where(local_slot < own_count, own_offset + local_slot, -1)
    columns = pooled
    widened_sum = jnp.dot(
        columns,
        lax.all_gather(up_weight, "seq", axis=0, tiled=True),
        preferred_element_type=jnp.float32,
    )
    widened_share = (widened_sum + up_bias[None, :]).astype(jnp.bfloat16)
    widened = lax.all_gather(widened_share, "mp", axis=1, tiled=True)
    inner_normed = rms_scale(widened, inner_gain).astype(jnp.bfloat16)
    columns = inner_normed
    query_part = jnp.dot(
        columns,
        lax.all_gather(query_weight, "seq", axis=0, tiled=True),
        preferred_element_type=jnp.float32,
    )
    key_part = jnp.dot(
        columns,
        lax.all_gather(key_weight, "seq", axis=0, tiled=True),
        preferred_element_type=jnp.float32,
    )
    value_part = jnp.dot(
        columns,
        lax.all_gather(value_weight, "seq", axis=0, tiled=True),
        preferred_element_type=jnp.float32,
    )
    queries = query_part.astype(jnp.bfloat16)
    key_rows = key_part.astype(jnp.bfloat16)
    value_rows = value_part.astype(jnp.bfloat16)
    query_count = queries.shape[0]
    grouped = (
        queries.reshape(query_count, kv_local, group_size, HEAD)
        .transpose(1, 0, 2, 3)
        .reshape(kv_local, query_count * group_size, HEAD)
    )
    row_index = jnp.repeat(query_index, group_size)
    shard_rows = key_rows.shape[0]
    score_scale = 1.0 / math.sqrt(HEAD)

    def key_index(whole_index):
        holder = whole_index // shard_rows
        within = whole_index % shard_rows
        holder_offset = pick_table(offsets, holder, seq_ids)
        holder_count = pick_table(span_counts, holder, seq_ids)
        return jnp.where(within < holder_count, holder_offset + within, far_index)

    def attend_block(running, key_block, value_block, index_block):
        row_peak, denominator, weighted = running
        scores = (
            jnp.einsum("hqd,khd->hqk", grouped, key_block, preferred_element_type=jnp.float32)
            * score_scale
        )
        scores = jnp.where(index_block[None, None, :] <= row_index[None, :, None], scores, masked)
        new_peak = jnp.maximum(row_peak, jnp.max(scores, axis=2))
        shrink = jnp.exp(row_peak - new_peak)
        lifted = jnp.exp(scores - new_peak[:, :, None])
        denominator = denominator * shrink + jnp.sum(lifted, axis=2)
        weighted = weighted * shrink[:, :, None] + jnp.einsum(
            "hqk,khd->hqd",
            lifted.astype(jnp.bfloat16),
            value_block,
            preferred_element_type=jnp.float32,
        )
        return (new_peak, denominator, weighted)

    query_total = query_count * group_size
    initial = (
        jnp.full((kv_local, query_total), masked, jnp.float32),
        jnp.zeros((kv_local, query_total), jnp.float32),
        jnp.zeros((kv_local, query_total, HEAD), jnp.float32),
    )
    key_piece = lax.all_gather(key_rows, "seq", axis=0, tiled=True)
    value_piece = lax.all_gather(value_rows, "seq", axis=0, tiled=True)
    piece_rows = key_piece.shape[0]
    block_rows = block_size(piece_rows, shard_rows)
    turn_count = piece_rows // block_rows
    key_blocks = key_piece.reshape(turn_count, block_rows, kv_local, HEAD)
    value_blocks = value_piece.reshape(turn_count, block_rows, kv_local, HEAD)

    def one_turn(turn_index, inner_running):
        whole_index = turn_index * block_rows + jnp.arange(block_rows, dtype=jnp.int32)
        return attend_block(
            inner_running, key_blocks[turn_index], value_blocks[turn_index], key_index(whole_index)
        )

    row_peak, denominator, weighted = lax.fori_loop(0, turn_count, one_turn, initial)
    attended = (weighted / denominator[:, :, None]).astype(jnp.bfloat16)
    attended = (
        attended.reshape(kv_local, query_count, group_size, HEAD)
        .transpose(1, 0, 2, 3)
        .reshape(query_count, kv_local * group_size * HEAD)
    )
    projected = jnp.dot(attended, return_weight, preferred_element_type=jnp.float32)
    returned = lax.psum_scatter(
        projected.astype(jnp.bfloat16), "mp", scatter_dimension=1, tiled=True
    )
    positions = jnp.arange(rows_here, dtype=jnp.int32)
    live_slots = jnp.arange(capacity, dtype=jnp.int32) < own_count
    passed = jnp.sum(
        ((own_marks[None, :] <= positions[:, None]) & live_slots[None, :]).astype(jnp.int32), axis=1
    )
    return (skip_part.astype(jnp.float32) + returned[passed - 1].astype(jnp.float32)).astype(
        jnp.bfloat16
    )


def solution(mesh):
    in_specs = (
        P("seq", None),
        P(),
        P(None, "mp"),
        P(None, "mp"),
        P("mp"),
        P("mp", None),
        P("seq", None),
        P(),
        P("seq", "mp"),
        P("mp"),
        P(),
        P("seq", "mp"),
        P("seq", "mp"),
        P("seq", "mp"),
        P("mp", None),
    )
    out_specs = P("seq", "mp")
    return jax.shard_map(
        on_device, mesh=mesh, in_specs=in_specs, out_specs=out_specs, check_vma=False
    )
```

profile of v0, /device:TPU:8, one launch (start us, length us, event | category | flops | bytes accessed | tf_op | source)
XLA Modules:
  0.0 1139.2 jit_solution(18261109659851616036)
XLA Ops:
  7.4 1.3 fusion.32
  8.8 1.5 negate_exponential_fusion
  12.6 79.6 %all-gather.1 = f32[64,1,128]{2,1,0:T(1,128)S(1)} all-gather(f32[1,1,128]{2,1,0:T(1,128)S(1)} %add_bitcast_fusion), channel_id=1, replica_groups=mesh['seq'=64,'mp'=8] {'seq'}, dimensions={0}, use_global_device_ids=true | all-gather | bytes 33280 | tf_op jit(solution)/shard_map/all_gather | solution.py:17
  92.3 73.3 %all-gather = f32[64,1,128]{2,1,0:T(1,128)S(1)} all-gather(f32[1,1,128]{2,1,0:T(1,128)S(1)} %add_bitcast_fusion.1), channel_id=1, replica_groups=mesh['seq'=64,'mp'=8] {'seq'}, dimensions={0}, use_global_device_ids=true | all-gather | bytes 33280 | tf_op jit(solution)/shard_map/all_gather | solution.py:17
  165.6 2.6 while.34
  168.2 1.3 fusion.43
  170.2 73.0 %all-reduce.34.cloned.1.call-done = f32[256,1024]{1,0:T(8,128)} async-done(((f32[256,1024]{1,0:T(8,128)}), f32[256,1024]{1,0:T(8,128)}) %all-reduce.34.cloned.1.call-update) | async-done | bytes 1048592 | tf_op jit(solution)/shard_map/psum | solution.py:92
  243.2 1.4 fusion.35
  244.6 0.9 gather_fusion
  245.5 61.3 %all-gather.10.cloned.1.call-done = bf16[1024,512]{1,0:T(8,128)(2,1)} async-done(((bf16[16,512]{1,0:T(8,128)(2,1)}), bf16[1024,512]{1,0:T(8,128)(2,1)}) %all-gather.10.cloned.1.call-update) | async-done | bytes 1048592 | tf_op jit(solution)/shard_map/all_gather | solution.py:102
  306.7 2.2 fusion.31
  310.9 26.2 %all-gather.12.cloned.1.call-done = bf16[128,4096]{1,0:T(8,128)(2,1)} async-done(((bf16[128,512]{1,0:T(8,128)(2,1)}), bf16[128,4096]{1,0:T(8,128)(2,1)}) %all-gather.12.cloned.1.call-update) | async-done | bytes 1048592 | tf_op jit(solution)/shard_map/all_gather | solution.py:106
  337.1 1.6 fusion.28
  338.8 140.2 %all-gather.20.cloned.1.call-done = bf16[4096,128]{1,0:T(8,128)(2,1)} async-done(((bf16[64,128]{1,0:T(8,128)(2,1)}), bf16[4096,128]{1,0:T(8,128)(2,1)}) %all-gather.20.cloned.1.call-update) | async-done | bytes 1048592 | tf_op jit(solution)/shard_map/all_gather | solution.py:121
  478.9 2.7 convolution_convert_fusion.2
  481.7 136.0 %all-gather.14.cloned.1.call-done = bf16[4096,128]{1,0:T(8,128)(2,1)} async-done(((bf16[64,128]{1,0:T(8,128)(2,1)}), bf16[4096,128]{1,0:T(8,128)(2,1)}) %all-gather.14.cloned.1.call-update) | async-done | bytes 1048592 | tf_op jit(solution)/shard_map/all_gather | solution.py:116
  617.7 2.3 convolution_convert_fusion.3
  620.5 1.3 fusion.50
  622.5 1.9 add_select_fusion.3
  625.1 137.2 %all-gather.18.cloned.1.call-done = bf16[4096,512]{1,0:T(8,128)(2,1)} async-done(((bf16[64,512]{1,0:T(8,128)(2,1)}), bf16[4096,512]{1,0:T(8,128)(2,1)}) %all-gather.18.cloned.1.call-update) | async-done | bytes 4194320 | tf_op jit(solution)/shard_map/all_gather | solution.py:111
  762.2 3.0 convolution_convert_fusion.1
  765.3 135.9 %all-gather.22.cloned.1.call-done = bf16[8192,128]{1,0:T(8,128)(2,1)} async-done(((bf16[128,128]{1,0:T(8,128)(2,1)}), bf16[8192,128]{1,0:T(8,128)(2,1)}) %all-gather.22.cloned.1.call-update) | async-done | bytes 2097168 | tf_op jit(solution)/shard_map/all_gather | solution.py:170
  901.2 140.0 %all-gather.16.cloned.1.call-done = bf16[8192,128]{1,0:T(8,128)(2,1)} async-done(((bf16[128,128]{1,0:T(8,128)(2,1)}), bf16[8192,128]{1,0:T(8,128)(2,1)}) %all-gather.16.cloned.1.call-update) | async-done | bytes 2097168 | tf_op jit(solution)/shard_map/all_gather | solution.py:169
  1041.2 50.0 %while.35 = (s32[]{:T(128)}, f32[1,512]{1,0:T(1,128)S(1)}, f32[1,512]{1,0:T(1,128)S(1)}, f32[1,512,128]{2,1,0:T(8,128)S(1)}, s32[64]{0:T(128)S(1)}, /*index=5*/s...) while((s32[]{:T(128)}, f32[1,512]{1,0:T(1,128)S(1)}, ...), condition=%wide.region_13.14_spmd.clone, body=%wide.region_8.13_spmd.clone.sunk | while | flops 273186304 | bytes 7548097 | solution.py:183
  1041.2 0.8 fusion.77
  1042.9 2.0 fusion.78
  1046.0 1.5 fusion.82
  1047.5 0.8 fusion.77
  1049.2 2.0 fusion.78
  1052.2 1.5 fusion.82
  1053.7 0.8 fusion.77
  1055.4 2.0 fusion.78
  1058.5 1.5 fusion.82
  1061.7 2.0 fusion.78
  1064.7 1.5 fusion.82
  1067.9 2.0 fusion.78
  1071.0 1.5 fusion.82
  1074.1 2.0 fusion.78
  1077.2 1.5 fusion.82
  1080.4 2.0 fusion.78
  1083.5 1.5 fusion.82
  1086.6 2.0 fusion.78
  1089.7 1.5 fusion.82
  1091.8 0.8 copy.28
  1092.7 35.8 %reduce-scatter.4.cloned.1.call-done = bf16[128,128]{1,0:T(8,128)(2,1)} async-done(((bf16[1024,128]{1,0:T(8,128)(2,1)}), bf16[128,128]{1,0:T(8,128)(2,1)}) %reduce-scatter.4.cloned.1.call-update) | async-done | bytes 32784
  1128.5 0.9 copy.29
  1129.4 0.9 gather_fusion.1
  1130.3 1.5 add_convert_fusion
  (335 shorter events, 27.5 us)
Async XLA Ops:
  7.4 1084.1 %copy-start = (bf16[512,1024]{1,0:T(8,128)(2,1)S(1)}, bf16[512,1024]{1,0:T(8,128)(2,1)}, u32[]{:S(2)}) copy-start(bf16[512,1024]{1,0:T(8,128)(2,1)} %param.33) | copy-start | bytes 3145732
  7.4 3.0 copy-start.2
  7.4 3.0 copy-start.12
  7.4 3.0 copy-start.10
  7.4 235.8 %all-reduce.34.cloned.1.call-start = ((), (), s32[]{:S(2)}) async-start(), calls=%async_computation.1 | async-start | bytes 2097152 | tf_op jit(solution)/shard_map/psum | solution.py:92
  11.7 156.5 %copy-start.4 = (bf16[128,1024]{1,0:T(8,128)(2,1)S(1)}, bf16[128,1024]{1,0:T(8,128)(2,1)}, u32[]{:S(2)}) copy-start(bf16[128,1024]{1,0:T(8,128)(2,1)} %param.24) | copy-start | bytes 786436
  12.5 157.6 %copy-start.9 = (s32[1,128]{1,0:T(1,128)S(1)}, s32[1,128]{1,0:T(1,128)}, u32[]{:S(2)}) copy-start(s32[1,128]{1,0:T(1,128)} %param.25) | copy-start | bytes 1540
  169.5 137.2 %all-gather.10.cloned.1.call-start = ((), (), s32[]{:S(2)}) async-start(), calls=%async_computation.2 | async-start | bytes 1064960 | tf_op jit(solution)/shard_map/all_gather | solution.py:102
  170.1 167.0 %all-gather.12.cloned.1.call-start = ((), (), s32[]{:S(2)}) async-start(), calls=%async_computation.3 | async-start | bytes 1179648 | tf_op jit(solution)/shard_map/all_gather | solution.py:106
  170.2 136.5 %copy-start.8 = (f32[512]{0:T(512)S(1)}, f32[512]{0:T(512)}, u32[]{:S(2)}) copy-start(f32[512]{0:T(512)} %param.28) | copy-start | bytes 6148
  244.6 94.2 %copy-start.1 = (bf16[256,1024]{1,0:T(8,128)(2,1)}, bf16[256,1024]{1,0:T(8,128)(2,1)S(1)}, u32[]{:S(2)}) copy-start(bf16[256,1024]{1,0:T(8,128)(2,1)S(1)} %fusion.35) | copy-start | bytes 1572868
  244.6 234.3 %copy-start.11 = (f32[4096]{0:T(1024)S(1)}, f32[4096]{0:T(1024)}, u32[]{:S(2)}) copy-start(f32[4096]{0:T(1024)} %param.29) | copy-start | bytes 49156
  309.0 170.0 %all-gather.20.cloned.1.call-start = ((), (), s32[]{:S(2)}) async-start(), calls=%async_computation.7 | async-start | bytes 1064960 | tf_op jit(solution)/shard_map/all_gather | solution.py:121
  309.7 308.0 %all-gather.14.cloned.1.call-start = ((), (), s32[]{:S(2)}) async-start(), calls=%async_computation.4 | async-start | bytes 1064960 | tf_op jit(solution)/shard_map/all_gather | solution.py:116
  310.3 452.0 %all-gather.18.cloned.1.call-start = ((), (), s32[]{:S(2)}) async-start(), calls=%async_computation.6 | async-start | bytes 4259840 | tf_op jit(solution)/shard_map/all_gather | solution.py:111
  310.9 590.4 %all-gather.22.cloned.1.call-start = ((), (), s32[]{:S(2)}) async-start(), calls=%async_computation.8 | async-start | bytes 2129920 | tf_op jit(solution)/shard_map/all_gather | solution.py:170
  337.1 280.6 %copy-start.3 = (bf16[128,4096]{1,0:T(8,128)(2,1)S(1)}, bf16[128,4096]{1,0:T(8,128)(2,1)}, u32[]{:S(2)}) copy-start(bf16[128,4096]{1,0:T(8,128)(2,1)} %all-gather.12.cloned.1.call-done) | copy-start | bytes 3145732
  338.8 281.4 %copy-start.5 = (s32[64]{0:T(128)S(1)}, s32[64]{0:T(128)}, u32[]{:S(2)}) copy-start(s32[64]{0:T(128)} %param.26) | copy-start | bytes 772
  481.6 559.6 %all-gather.16.cloned.1.call-start = ((), (), s32[]{:S(2)}) async-start(), calls=%async_computation.5 | async-start | bytes 2129920 | tf_op jit(solution)/shard_map/all_gather | solution.py:169
  620.1 508.4 %reduce-scatter.4.cloned.1.call-start = ((), (), s32[]{:S(2)}) async-start(), calls=%async_computation.9 | async-start | bytes 294912
  1045.6 1.9 copy-start.6
  1051.8 1.9 copy-start.6
  1058.1 1.9 copy-start.6
  1064.3 1.9 copy-start.6
  1070.6 1.9 copy-start.6
  1076.8 1.9 copy-start.6
  1083.1 1.9 copy-start.6
  1089.3 1.9 copy-start.6
  1091.2 1.4 copy-start.7
Sparse Core Ops, SparseCore 0:
  169.7 73.5 all-reduce.33
  309.1 27.9 all-gather.11
  340.1 138.8 all-gather.19
  481.7 135.9 all-gather.13
  620.5 141.6 all-gather.17
  765.0 136.1 all-gather.21
  904.2 137.0 all-gather.15
  1092.8 35.7 reduce-scatter.3
Sparse Core Ops, SparseCore 1:
  173.0 133.7 all-gather.9
where the time goes:
time: 1140 us
  waiting for transfers between devices  888 us (78%)
  blocking collectives  153 us (13%)
  matrix products  41.2 us (4%)
  other arithmetic  27.3 us (2%)
  between operations  15.9 us (1%)
  local copies, waits for them, and re-layouts  11.6 us (1%)
    all_gather x2, blocking collectives, prefix(): pieces = jax.tree.map(lambda part: lax.all_gather(part, axis), value)  153 us
    all_gather x1, waiting for transfers between devices, on_device(): lax.all_gather(value_weight, 'seq', axis=0, tiled=True)  140 us
    all_gather x1, waiting for transfers between devices, on_device(): key_piece = lax.all_gather(key_rows, 'seq', axis=0, tiled=True)  140 us
    all_gather x1, waiting for transfers between devices, on_device(): lax.all_gather(query_weight, 'seq', axis=0, tiled=True)  137 us
    all_gather x1, waiting for transfers between devices, on_device(): lax.all_gather(key_weight, 'seq', axis=0, tiled=True)  136 us
    all_gather x1, waiting for transfers between devices, on_device(): value_piece = lax.all_gather(value_rows, 'seq', axis=0, tiled=True)  136 us
    psum x1, waiting for transfers between devices, on_device(): mixed_sum = lax.psum(partial_value, 'mp')  73 us
    all_gather x1, waiting for transfers between devices, on_device(): lax.all_gather(up_weight, 'seq', axis=0, tiled=True)  61.3 us
  transfers between devices with their start and end apart: 9, of which 9 were waited for; matrix products, arithmetic and copies ran while one was open for 1% of the time, Pallas kernels for 0%

commit v1 on v0

--- a/solution.py
+++ b/solution.py
@@ -89,7 +89,7 @@
     arriving = prefix((through[-1], local_states[-1]), "seq", combine_pairs, starting)
     states = (local_states + through * arriving[1][None, :]).astype(jnp.bfloat16)
     partial_value = jnp.dot(states, mixer_weight, preferred_element_type=jnp.float32)
-    mixed_sum = lax.psum(partial_value, "mp")
+    mixed_sum = jnp.sum(lax.all_gather(partial_value, "mp"), axis=0)
     encoded = (byte_states.astype(jnp.float32) + mixed_sum).astype(jnp.bfloat16)
     skip_part = lax.dynamic_slice_in_dim(encoded, own_lane * column_count, column_count, 1)
     own_marks = boundaries[0]

time: 1140 us -> 1200 us (1.053)
  waiting for transfers between devices: 888 us -> 942 us
    all_gather x1, waiting for transfers between devices: 61.3 us -> 137 us  [on_device(): lax.all_gather(up_weight, 'seq', axis=0, tiled=True)]
    psum x1 -> x0, waiting for transfers between devices: 73 us -> none  [on_device(): mixed_sum = lax.psum(partial_value, 'mp')]
    all_gather x0 -> x1, waiting for transfers between devices: none -> 51.4 us  [on_device(): mixed_sum = jnp.sum(lax.all_gather(partial_value, 'mp'), axis=0)]
  transfers between devices with their start and end apart: 9 -> 9, of which waited for: 9 -> 9; matrix products, arithmetic and copies ran while one was open for 1% -> 2% of each run, Pallas kernels for 0% -> 0%
where the time goes in v1:
time: 1200 us; the launch traced here: 1190 us
  waiting for transfers between devices  942 us (78%)
  blocking collectives  153 us (13%)
  matrix products  41.2 us (3%)
  other arithmetic  29.8 us (2%)
  between operations  14.2 us (1%)
    all_gather x2, blocking collectives, prefix(): pieces = jax.tree.map(lambda part: lax.all_gather(part, axis), value)  153 us
    all_gather x1, waiting for transfers between devices, on_device(): lax.all_gather(value_weight, 'seq', axis=0, tiled=True)  140 us
    all_gather x1, waiting for transfers between devices, on_device(): key_piece = lax.all_gather(key_rows, 'seq', axis=0, tiled=True)  140 us
    all_gather x1, waiting for transfers between devices, on_device(): lax.all_gather(query_weight, 'seq', axis=0, tiled=True)  138 us
    all_gather x1, waiting for transfers between devices, on_device(): lax.all_gather(up_weight, 'seq', axis=0, tiled=True)  137 us
    all_gather x1, waiting for transfers between devices, on_device(): value_piece = lax.all_gather(value_rows, 'seq', axis=0, tiled=True)  136 us
    all_gather x1, waiting for transfers between devices, on_device(): lax.all_gather(key_weight, 'seq', axis=0, tiled=True)  136 us
    all_gather x1, waiting for transfers between devices, on_device(): mixed_sum = jnp.sum(lax.all_gather(partial_value, 'mp'), axis=0)  51.4 us
  transfers between devices with their start and end apart: 9, of which 9 were waited for; matrix products, arithmetic and copies ran while one was open for 2% of the time, Pallas kernels for 0%

profile of v1, /device:TPU:8, one launch (start us, length us, event | category | flops | bytes accessed | tf_op | source)
XLA Modules:
  0.0 1193.9 jit_solution(5243397036859866671)
XLA Ops:
  6.6 1.3 fusion.32
  7.9 1.5 negate_exponential_fusion
  11.8 79.6 %all-gather.2 = f32[64,1,128]{2,1,0:T(1,128)S(1)} all-gather(f32[1,1,128]{2,1,0:T(1,128)S(1)} %add_bitcast_fusion), channel_id=1, replica_groups=mesh['seq'=64,'mp'=8] {'seq'}, dimensions={0}, use_global_device_ids=true | all-gather | bytes 33280 | tf_op jit(solution)/shard_map/all_gather | solution.py:17
  91.5 73.3 %all-gather.1 = f32[64,1,128]{2,1,0:T(1,128)S(1)} all-gather(f32[1,1,128]{2,1,0:T(1,128)S(1)} %add_bitcast_fusion.1), channel_id=1, replica_groups=mesh['seq'=64,'mp'=8] {'seq'}, dimensions={0}, use_global_device_ids=true | all-gather | bytes 33280 | tf_op jit(solution)/shard_map/all_gather | solution.py:17
  164.8 2.6 while.34
  167.4 1.3 fusion.43
  169.5 51.4 %all-gather.26.cloned.1.call-done = f32[2048,1024]{1,0:T(8,128)} async-done(((f32[256,1024]{1,0:T(8,128)}), f32[2048,1024]{1,0:T(8,128)}) %all-gather.26.cloned.1.call-update) | async-done | bytes 8388624 | tf_op jit(solution)/shard_map/all_gather | solution.py:92
  221.0 4.4 reduce_sum.100
  225.5 0.9 gather_fusion
  226.4 136.7 %all-gather.12.cloned.1.call-done = bf16[1024,512]{1,0:T(8,128)(2,1)} async-done(((bf16[16,512]{1,0:T(8,128)(2,1)}), bf16[1024,512]{1,0:T(8,128)(2,1)}) %all-gather.12.cloned.1.call-update) | async-done | bytes 1048592 | tf_op jit(solution)/shard_map/all_gather | solution.py:102
  363.1 2.2 fusion.31
  367.1 26.3 %all-gather.14.cloned.1.call-done = bf16[128,4096]{1,0:T(8,128)(2,1)} async-done(((bf16[128,512]{1,0:T(8,128)(2,1)}), bf16[128,4096]{1,0:T(8,128)(2,1)}) %all-gather.14.cloned.1.call-update) | async-done | bytes 1048592 | tf_op jit(solution)/shard_map/all_gather | solution.py:106
  393.4 1.6 fusion.28
  395.1 140.0 %all-gather.22.cloned.1.call-done = bf16[4096,128]{1,0:T(8,128)(2,1)} async-done(((bf16[64,128]{1,0:T(8,128)(2,1)}), bf16[4096,128]{1,0:T(8,128)(2,1)}) %all-gather.22.cloned.1.call-update) | async-done | bytes 1048592 | tf_op jit(solution)/shard_map/all_gather | solution.py:121
  535.1 2.7 convolution_convert_fusion.2
  537.8 136.0 %all-gather.16.cloned.1.call-done = bf16[4096,128]{1,0:T(8,128)(2,1)} async-done(((bf16[64,128]{1,0:T(8,128)(2,1)}), bf16[4096,128]{1,0:T(8,128)(2,1)}) %all-gather.16.cloned.1.call-update) | async-done | bytes 1048592 | tf_op jit(solution)/shard_map/all_gather | solution.py:116
  673.9 2.4 convolution_convert_fusion.3
  676.6 1.2 fusion.50
  678.5 1.7 add_select_fusion.3
  680.9 137.5 %all-gather.20.cloned.1.call-done = bf16[4096,512]{1,0:T(8,128)(2,1)} async-done(((bf16[64,512]{1,0:T(8,128)(2,1)}), bf16[4096,512]{1,0:T(8,128)(2,1)}) %all-gather.20.cloned.1.call-update) | async-done | bytes 4194320 | tf_op jit(solution)/shard_map/all_gather | solution.py:111
  818.4 2.9 convolution_convert_fusion.1
  821.4 136.1 %all-gather.24.cloned.1.call-done = bf16[8192,128]{1,0:T(8,128)(2,1)} async-done(((bf16[128,128]{1,0:T(8,128)(2,1)}), bf16[8192,128]{1,0:T(8,128)(2,1)}) %all-gather.24.cloned.1.call-update) | async-done | bytes 2097168 | tf_op jit(solution)/shard_map/all_gather | solution.py:170
  957.5 140.0 %all-gather.18.cloned.1.call-done = bf16[8192,128]{1,0:T(8,128)(2,1)} async-done(((bf16[128,128]{1,0:T(8,128)(2,1)}), bf16[8192,128]{1,0:T(8,128)(2,1)}) %all-gather.18.cloned.1.call-update) | async-done | bytes 2097168 | tf_op jit(solution)/shard_map/all_gather | solution.py:169
  1097.5 49.3 %while.35 = (s32[]{:T(128)}, f32[1,512]{1,0:T(1,128)S(1)}, f32[1,512]{1,0:T(1,128)S(1)}, f32[1,512,128]{2,1,0:T(8,128)S(1)}, s32[64]{0:T(128)S(1)}, /*index=5*/s...) while((s32[]{:T(128)}, f32[1,512]{1,0:T(1,128)S(1)}, ...), condition=%wide.region_13.14_spmd.clone, body=%wide.region_8.13_spmd.clone.sunk | while | flops 273186304 | bytes 7548097 | solution.py:183
  1097.5 0.7 fusion.77
  1099.1 2.0 fusion.78
  1102.2 1.5 fusion.82
  1105.3 2.0 fusion.78
  1108.4 1.5 fusion.82
  1111.5 2.0 fusion.78
  1114.5 1.5 fusion.82
  1117.6 2.0 fusion.78
  1120.7 1.5 fusion.82
  1123.8 2.0 fusion.78
  1126.9 1.5 fusion.82
  1128.4 0.7 fusion.77
  1130.0 2.0 fusion.78
  1133.0 1.5 fusion.82
  1134.5 0.7 fusion.77
  1136.1 2.0 fusion.78
  1139.2 1.5 fusion.82
  1142.3 2.0 fusion.78
  1145.4 1.5 fusion.82
  1147.4 0.8 copy.28
  1148.3 35.8 %reduce-scatter.4.cloned.1.call-done = bf16[128,128]{1,0:T(8,128)(2,1)} async-done(((bf16[1024,128]{1,0:T(8,128)(2,1)}), bf16[128,128]{1,0:T(8,128)(2,1)}) %reduce-scatter.4.cloned.1.call-update) | async-done | bytes 32784
  1184.2 0.9 copy.29
  1185.0 0.9 gather_fusion.1
  1185.9 1.5 add_convert_fusion
  (336 shorter events, 27.0 us)
Async XLA Ops:
  6.5 1140.6 %copy-start = (bf16[512,1024]{1,0:T(8,128)(2,1)S(1)}, bf16[512,1024]{1,0:T(8,128)(2,1)}, u32[]{:S(2)}) copy-start(bf16[512,1024]{1,0:T(8,128)(2,1)} %param.33) | copy-start | bytes 3145732
  6.5 3.0 copy-start.2
  6.5 3.0 copy-start.12
  6.5 3.0 copy-start.10
  6.5 214.4 %all-gather.26.cloned.1.call-start = ((), (), s32[]{:S(2)}) async-start(), calls=%async_computation.8 | async-start | bytes 9437184 | tf_op jit(solution)/shard_map/all_gather | solution.py:92
  10.9 156.5 %copy-start.4 = (bf16[128,1024]{1,0:T(8,128)(2,1)S(1)}, bf16[128,1024]{1,0:T(8,128)(2,1)}, u32[]{:S(2)}) copy-start(bf16[128,1024]{1,0:T(8,128)(2,1)} %param.24) | copy-start | bytes 786436
  11.7 157.8 %copy-start.9 = (s32[1,128]{1,0:T(1,128)S(1)}, s32[1,128]{1,0:T(1,128)}, u32[]{:S(2)}) copy-start(s32[1,128]{1,0:T(1,128)} %param.25) | copy-start | bytes 1540
  168.7 194.4 %all-gather.12.cloned.1.call-start = ((), (), s32[]{:S(2)}) async-start(), calls=%async_computation.1 | async-start | bytes 1064960 | tf_op jit(solution)/shard_map/all_gather | solution.py:102
  169.5 224.0 %all-gather.14.cloned.1.call-start = ((), (), s32[]{:S(2)}) async-start(), calls=%async_computation.2 | async-start | bytes 1179648 | tf_op jit(solution)/shard_map/all_gather | solution.py:106
  225.4 137.7 %copy-start.8 = (f32[512]{0:T(512)S(1)}, f32[512]{0:T(512)}, u32[]{:S(2)}) copy-start(f32[512]{0:T(512)} %param.28) | copy-start | bytes 6148
  225.5 169.5 %copy-start.1 = (bf16[256,1024]{1,0:T(8,128)(2,1)}, bf16[256,1024]{1,0:T(8,128)(2,1)S(1)}, u32[]{:S(2)}) copy-start(bf16[256,1024]{1,0:T(8,128)(2,1)S(1)} %fusion.35) | copy-start | bytes 1572868
  225.5 309.6 %copy-start.11 = (f32[4096]{0:T(1024)S(1)}, f32[4096]{0:T(1024)}, u32[]{:S(2)}) copy-start(f32[4096]{0:T(1024)} %param.29) | copy-start | bytes 49156
  365.3 169.8 %all-gather.22.cloned.1.call-start = ((), (), s32[]{:S(2)}) async-start(), calls=%async_computation.6 | async-start | bytes 1064960 | tf_op jit(solution)/shard_map/all_gather | solution.py:121
  365.9 308.0 %all-gather.16.cloned.1.call-start = ((), (), s32[]{:S(2)}) async-start(), calls=%async_computation.3 | async-start | bytes 1064960 | tf_op jit(solution)/shard_map/all_gather | solution.py:116
  366.5 451.9 %all-gather.20.cloned.1.call-start = ((), (), s32[]{:S(2)}) async-start(), calls=%async_computation.5 | async-start | bytes 4259840 | tf_op jit(solution)/shard_map/all_gather | solution.py:111
  367.1 590.5 %all-gather.24.cloned.1.call-start = ((), (), s32[]{:S(2)}) async-start(), calls=%async_computation.7 | async-start | bytes 2129920 | tf_op jit(solution)/shard_map/all_gather | solution.py:170
  393.4 280.4 %copy-start.3 = (bf16[128,4096]{1,0:T(8,128)(2,1)S(1)}, bf16[128,4096]{1,0:T(8,128)(2,1)}, u32[]{:S(2)}) copy-start(bf16[128,4096]{1,0:T(8,128)(2,1)} %all-gather.14.cloned.1.call-done) | copy-start | bytes 3145732
  395.1 281.3 %copy-start.5 = (s32[64]{0:T(128)S(1)}, s32[64]{0:T(128)}, u32[]{:S(2)}) copy-start(s32[64]{0:T(128)} %param.26) | copy-start | bytes 772
  537.8 559.7 %all-gather.18.cloned.1.call-start = ((), (), s32[]{:S(2)}) async-start(), calls=%async_computation.4 | async-start | bytes 2129920 | tf_op jit(solution)/shard_map/all_gather | solution.py:169
  676.3 507.9 %reduce-scatter.4.cloned.1.call-start = ((), (), s32[]{:S(2)}) async-start(), calls=%async_computation.9 | async-start | bytes 294912
  1101.8 1.9 copy-start.6
  1108.0 1.9 copy-start.6
  1114.1 1.9 copy-start.6
  1120.3 1.9 copy-start.6
  1126.5 1.9 copy-start.6
  1132.6 1.9 copy-start.6
  1138.8 1.9 copy-start.6
  1145.0 1.9 copy-start.6
  1146.8 1.5 copy-start.7
Sparse Core Ops, SparseCore 0:
  168.8 52.0 all-gather.25
  223.9 139.1 all-gather.11
  365.4 27.9 all-gather.13
  396.2 138.8 all-gather.21
  537.9 135.9 all-gather.15
  676.7 141.6 all-gather.19
  821.3 136.1 all-gather.23
  960.5 137.0 all-gather.17
  1148.4 35.7 reduce-scatter.3
